TPU v7x, 256 devices: a whole 4x4x8 slice. The times are simulated.
256 devices in a mesh: dp: 4 (over x), seq: 8 (over z_lo, y), tensor: 8 (over z_hi, core).
Axes of the slice: x: 4, y: 4, z: 8 (z_hi: 4, z_lo: 2; z = z_hi * 2 + z_lo), core: 2. Of those that a mesh axis runs over, the one named last changes fastest.
Arguments:
- hidden: bfloat16 [4096, 28672], P(('dp', 'seq'), 'tensor'), may hold values from -6 to 6
- weight: bfloat16 [28672, 4096], P('tensor', 'seq'), may hold values from -0.03125 to 0.03125
- out_grad: bfloat16 [4096, 4096], P(('dp', 'tensor'), 'seq'), may hold values from -6 to 6
Outputs:
- output: bfloat16 [4096, 4096], P(('dp', 'tensor'), 'seq')
- grad_hidden: bfloat16 [4096, 28672], P(('dp', 'seq'), 'tensor')
- grad_weight: bfloat16 [28672, 4096], P('tensor', 'seq')
All inputs are finite; a program needn't handle non-finite values.
Results may differ from a plain program's by a relative error of at most 0.017.
Values may be sent and summed in bfloat16 or wider, within the bound.
A program may use at most 128 MiB of HBM per device.

v0:
```python
import jax
import jax.numpy as jnp
from jax import lax
from jax.sharding import PartitionSpec as P

HB = 512


def partner_2(shard, axis, distance):
    return lax.ppermute(shard, axis, [(i, i ^ 1 << distance) for i in range(lax.axis_size(axis))])


def walsh_table(table_order):
    matrix = jnp.ones((1, 1), jnp.float32)
    while matrix.shape[0] < table_order:
        matrix = jnp.concatenate(
            [jnp.concatenate([matrix, matrix], 1), jnp.concatenate([matrix, -matrix], 1)], 0
        )
    return matrix


def local_blocks(values, inner_table):
    row_count, feature_count = values.shape
    block_size = inner_table.shape[0]
    shaped = values.reshape(row_count, feature_count // block_size, block_size)
    if values.dtype == jnp.bfloat16:
        mixed_rows = jnp.einsum(
            "rbk,kl->rbl",
            shaped,
            inner_table.astype(jnp.bfloat16),
            preferred_element_type=jnp.float32,
        )
    else:
        mixed_rows = jnp.einsum("rbk,kl->rbl", shaped, inner_table, precision=lax.Precision.HIGHEST)
    return mixed_rows.reshape(row_count, feature_count)


def butterfly(values):
    axis_count = lax.axis_size("tensor")
    device_index = lax.axis_index("tensor")
    for bit_index in range(axis_count.bit_length() - 1):
        partner = partner_2(values.astype(jnp.bfloat16), "tensor", bit_index).astype(values.dtype)
        upper_half = device_index // (1 << bit_index) % 2 == 1
        values = jnp.where(upper_half, partner - values, values + partner)
    return values


def rotate(values, inner_table, norm_scale):
    return (butterfly(local_blocks(values, inner_table)) * norm_scale).astype(jnp.bfloat16)


def body(hidden, weight, out_grad):
    inner_table = walsh_table(HB)
    norm_scale = 1.0 / float(lax.axis_size("tensor") * HB) ** 0.5
    rotated = rotate(hidden, inner_table, norm_scale)
    gathered = lax.all_gather(rotated, "seq", axis=0, tiled=True)
    partial_sums = jnp.dot(gathered, weight, preferred_element_type=jnp.float32)
    output = lax.psum_scatter(
        partial_sums.astype(jnp.bfloat16), "tensor", scatter_dimension=0, tiled=True
    )
    grads_all = lax.all_gather(out_grad, "tensor", axis=0, tiled=True)
    token_total = hidden.shape[0] * lax.axis_size("seq") * lax.axis_size("dp")
    grad_term = lax.dot_general(
        gathered, grads_all, (((0,), (0,)), ((), ())), preferred_element_type=jnp.float32
    )
    grad_weight = lax.psum(
        (grad_term * (1.0 / float(token_total) ** 0.5)).astype(jnp.bfloat16), "dp"
    )
    rotated_grad = lax.psum_scatter(
        lax.dot_general(
            grads_all, weight, (((1,), (1,)), ((), ())), preferred_element_type=jnp.float32
        ).astype(jnp.bfloat16),
        "seq",
        scatter_dimension=0,
        tiled=True,
    ).astype(jnp.float32)
    grad_hidden = rotate(rotated_grad, inner_table, norm_scale)
    return (output, grad_hidden, grad_weight)


def solution(mesh):
    in_specs = (P(("dp", "seq"), "tensor"), P("tensor", "seq"), P(("dp", "tensor"), "seq"))
    out_specs = (P(("dp", "tensor"), "seq"), P(("dp", "seq"), "tensor"), P("tensor", "seq"))
    return jax.shard_map(body, mesh=mesh, in_specs=in_specs, out_specs=out_specs, check_vma=False)
```

profile of v0, /device:TPU:1, one launch (start us, length us, event | category | flops | bytes accessed | tf_op | source)
XLA Modules:
  0.0 447.1 jit_solution(14021014759159372248)
XLA Ops:
  7.2 0.0 all-gather.5.cloned.1.call-start
  7.2 0.7 all-gather.5.cloned.1.call-update
  7.9 0.0 reduce-scatter.5.cloned.1.call-start
  7.9 36.3 %all-gather.5.cloned.1.call-done = bf16[1024,512]{1,0:T(8,128)(2,1)} async-done(((bf16[128,512]{1,0:T(8,128)(2,1)}), bf16[1024,512]{1,0:T(8,128)(2,1)}) %all-gather.5.cloned.1.call-update) | async-done | bytes 1048592 | tf_op jit(solution)/shard_map/all_gather | solution.py:61
  44.2 9.3 %convolution_convert_fusion = bf16[1024,3584]{1,0:T(8,128)(2,1)} fusion(bf16[1024,512]{1,0:T(8,128)(2,1)} %all-gather.5.cloned.1.call-done, bf16[3584,512]{1,0:T(8,128)(2,1)} %param.4), kind=kOutput, calls=%fused_computation | convolution fusion | flops 3761766400 | bytes 12058624 | tf_op jit(solution)/shard_map/dot_general | solution.py:70
  53.5 0.0 reduce-scatter.5.cloned.1.call-update
  53.6 0.0 copy-start.1
  53.6 0.0 all-gather.3.cloned.1.call-start
  53.6 1.1 copy-done
  54.7 0.6 copy.11
  55.3 0.0 copy-done.1
  55.3 0.7 fusion.14
  56.0 1.0 bitcast_convert_fusion.1
  57.1 0.3 collective-permute-start
  57.4 2.4 collective-permute-done
  59.7 1.2 fusion.13
  61.0 1.6 collective-permute-start.1
  62.5 41.3 %collective-permute-done.1 = bf16[128,3584]{0,1:T(8,128)(2,1)} collective-permute-done((bf16[128,3584]{0,1:T(8,128)(2,1)}, bf16[128,3584]{0,1:T(8,128)(2,1)}, u32[]{:S(2)}, u32[]{:S(2)}) %collective-permute-start.1) | collective-permute-done | bytes 917536 | tf_op jit(solution)/shard_map/ppermute | solution.py:10
  103.8 2.6 fusion.11
  106.5 2.7 collective-permute-start.2
  109.2 62.5 %collective-permute-done.2 = bf16[128,3584]{0,1:T(8,128)(2,1)} collective-permute-done((bf16[128,3584]{0,1:T(8,128)(2,1)}, bf16[128,3584]{0,1:T(8,128)(2,1)}, u32[]{:S(2)}, u32[]{:S(2)}) %collective-permute-start.2) | collective-permute-done | bytes 917536 | tf_op jit(solution)/shard_map/ppermute | solution.py:10
  171.7 3.2 fusion.4
  174.9 0.0 all-gather.3.cloned.1.call-update
  175.0 0.0 reduce-scatter.3.cloned.1.call-start
  175.0 20.5 %reduce-scatter.5.cloned.1.call-done = bf16[128,3584]{1,0:T(8,128)(2,1)} async-done(((bf16[1024,3584]{1,0:T(8,128)(2,1)}), bf16[128,3584]{1,0:T(8,128)(2,1)}) %reduce-scatter.5.cloned.1.call-update) | async-done | bytes 917520 | tf_op jit(solution)/shard_map/reduce_scatter | solution.py:69
  195.5 1.5 copy.13
  197.0 3.1 fusion.15
  200.1 1.0 bitcast_convert_fusion
  201.1 0.4 collective-permute-start.3
  201.5 79.5 %all-gather.3.cloned.1.call-done = bf16[1024,3584]{0,1:T(8,128)(2,1)} async-done(((bf16[128,3584]{0,1:T(8,128)(2,1)}), bf16[1024,3584]{0,1:T(8,128)(2,1)}) %all-gather.3.cloned.1.call-update) | async-done | bytes 7340048 | tf_op jit(solution)/shard_map/all_gather | solution.py:56
  281.0 9.1 %convolution_convert_fusion.1 = bf16[1024,512]{1,0:T(8,128)(2,1)} fusion(bf16[1024,3584]{0,1:T(8,128)(2,1)} %all-gather.3.cloned.1.call-done, bf16[3584,512]{1,0:T(8,128)(2,1)} %param.4), kind=kOutput, calls=%fused_computation.26 | convolution fusion | flops 3758620672 | bytes 12058624 | tf_op jit(solution)/shard_map/dot_general | solution.py:57
  290.1 0.0 reduce-scatter.3.cloned.1.call-update
  290.1 0.0 all-reduce.2.cloned.1.call-start
  290.2 0.0 copy-start.2
  290.2 0.0 collective-permute-done.3
  290.2 1.2 fusion.12
  291.4 2.3 collective-permute-start.4
  293.7 0.0 copy-done.2
  293.7 8.5 %multiply_convert_fusion = bf16[3584,512]{1,0:T(8,128)(2,1)} fusion(bf16[1024,3584]{0,1:T(8,128)(2,1)} %all-gather.3.cloned.1.call-done, bf16[1024,512]{1,0:T(8,128)(2,1)S(1)} %copy-done.2), kind=kOutput, calls=%fused_computation.1 | convolution fusion | flops 3761766400 | bytes 12058624 | tf_op jit(solution)/shard_map/dot_general | solution.py:63
  302.2 0.0 all-reduce.2.cloned.1.call-update
  302.2 41.2 %collective-permute-done.4 = bf16[128,3584]{0,1:T(8,128)(2,1)} collective-permute-done((bf16[128,3584]{0,1:T(8,128)(2,1)}, bf16[128,3584]{0,1:T(8,128)(2,1)}, u32[]{:S(2)}, u32[]{:S(2)}) %collective-permute-start.4) | collective-permute-done | bytes 917536 | tf_op jit(solution)/shard_map/ppermute | solution.py:10
  343.4 1.7 fusion.10
  345.1 6.5 %collective-permute-start.5 = (bf16[128,3584]{0,1:T(8,128)(2,1)S(1)}, bf16[128,3584]{0,1:T(8,128)(2,1)S(1)}, u32[]{:S(2)}, u32[]{:S(2)}) collective-permute-start(bf16[128,3584]{0,1:T(8,128)(2,1)S(1)} %fusion.10), channel_id=1, source_target_pairs={{0,4},{1,5},{2,6},{3,7},{4,0},{5,1},{6,2},{7,3},{8,12},{9,13},{10,... | collective-permute-start | bytes 2752520 | tf_op jit(solution)/shard_map/ppermute | solution.py:10
  351.6 40.0 %collective-permute-done.5 = bf16[128,3584]{0,1:T(8,128)(2,1)S(1)} collective-permute-done((bf16[128,3584]{0,1:T(8,128)(2,1)S(1)}, bf16[128,3584]{0,1:T(8,128)(2,1)S(1)}, u32[]{:S(2)}, u32[]{:S(2)}) %collective-permute-start.5) | collective-permute-done | bytes 917536 | tf_op jit(solution)/shard_map/ppermute | solution.py:10
  391.6 3.0 fusion.9
  394.6 2.2 copy.16
  396.8 39.6 %all-reduce.2.cloned.1.call-done = bf16[3584,512]{1,0:T(8,128)(2,1)} async-done(((bf16[3584,512]{1,0:T(8,128)(2,1)}), bf16[3584,512]{1,0:T(8,128)(2,1)}) %all-reduce.2.cloned.1.call-update) | async-done | bytes 3670032 | tf_op jit(solution)/shard_map/psum | solution.py:66
  436.4 4.1 copy.21
  (2 shorter events, 0.0 us)
Async XLA Ops:
  7.2 37.1 %all-gather.5.cloned.1.call-start = ((), (), s32[]{:S(2)}) async-start(), calls=%async_computation.4 | async-start | bytes 1179648 | tf_op jit(solution)/shard_map/all_gather | solution.py:61
  7.9 187.6 %reduce-scatter.5.cloned.1.call-start = ((), (), s32[]{:S(2)}) async-start(), calls=%async_computation.5 | async-start | bytes 8257536 | tf_op jit(solution)/shard_map/reduce_scatter | solution.py:69
  53.5 1.2 copy-start
  53.6 1.8 copy-start.1
  53.6 227.5 %all-gather.3.cloned.1.call-start = ((), (), s32[]{:S(2)}) async-start(), calls=%async_computation.2 | async-start | bytes 8257536 | tf_op jit(solution)/shard_map/all_gather | solution.py:56
  57.1 2.7 collective-permute-start
  61.0 42.9 %collective-permute-start.1 = (bf16[128,3584]{0,1:T(8,128)(2,1)}, bf16[128,3584]{0,1:T(8,128)(2,1)}, u32[]{:S(2)}, u32[]{:S(2)}) collective-permute-start(bf16[128,3584]{0,1:T(8,128)(2,1)} %fusion.13), channel_id=1, source_target_pairs={{0,2},{1,3},{2,0},{3,1},{4,6},{5,7},{6,4},{7,5},{8,10},{9,11},{10,... | collective-permute-start | bytes 2752520 | tf_op jit(solution)/shard_map/ppermute | solution.py:10
  106.5 65.2 %collective-permute-start.2 = (bf16[128,3584]{0,1:T(8,128)(2,1)}, bf16[128,3584]{0,1:T(8,128)(2,1)}, u32[]{:S(2)}, u32[]{:S(2)}) collective-permute-start(bf16[128,3584]{0,1:T(8,128)(2,1)} %fusion.11), channel_id=1, source_target_pairs={{0,4},{1,5},{2,6},{3,7},{4,0},{5,1},{6,2},{7,3},{8,12},{9,13},{10,... | collective-permute-start | bytes 2752520 | tf_op jit(solution)/shard_map/ppermute | solution.py:10
  175.0 221.8 %reduce-scatter.3.cloned.1.call-start = ((), (), s32[]{:S(2)}) async-start(), calls=%async_computation.3 | async-start | bytes 1179648 | tf_op jit(solution)/shard_map/reduce_scatter | solution.py:58
  201.1 89.1 %collective-permute-start.3 = (bf16[128,3584]{0,1:T(8,128)(2,1)}, bf16[128,3584]{0,1:T(8,128)(2,1)S(1)}, u32[]{:S(2)}, u32[]{:S(2)}) collective-permute-start(bf16[128,3584]{0,1:T(8,128)(2,1)} %bitcast_convert_fusion), channel_id=1, source_target_pairs={{0,1},{1,0},{2,3},{3,2},{4,5},{5,4},{6,7},{7,6},{8,9},{9,8},{10,11... | collective-permute-start | bytes 2752520 | tf_op jit(solution)/shard_map/ppermute | solution.py:10
  290.1 146.3 %all-reduce.2.cloned.1.call-start = ((), (), s32[]{:S(2)}) async-start(), calls=%async_computation.6 | async-start | bytes 7340032 | tf_op jit(solution)/shard_map/psum | solution.py:66
  290.2 3.5 copy-start.2
  291.4 52.0 %collective-permute-start.4 = (bf16[128,3584]{0,1:T(8,128)(2,1)}, bf16[128,3584]{0,1:T(8,128)(2,1)}, u32[]{:S(2)}, u32[]{:S(2)}) collective-permute-start(bf16[128,3584]{0,1:T(8,128)(2,1)} %fusion.12), channel_id=1, source_target_pairs={{0,2},{1,3},{2,0},{3,1},{4,6},{5,7},{6,4},{7,5},{8,10},{9,11},{10,... | collective-permute-start | bytes 2752520 | tf_op jit(solution)/shard_map/ppermute | solution.py:10
  345.1 46.4 %collective-permute-start.5 = (bf16[128,3584]{0,1:T(8,128)(2,1)S(1)}, bf16[128,3584]{0,1:T(8,128)(2,1)S(1)}, u32[]{:S(2)}, u32[]{:S(2)}) collective-permute-start(bf16[128,3584]{0,1:T(8,128)(2,1)S(1)} %fusion.10), channel_id=1, source_target_pairs={{0,4},{1,5},{2,6},{3,7},{4,0},{5,1},{6,2},{7,3},{8,12},{9,13},{10,... | collective-permute-start | bytes 2752520 | tf_op jit(solution)/shard_map/ppermute | solution.py:10
Sparse Core Ops, SparseCore 0:
  9.8 34.3 all-gather.4
  53.7 141.7 reduce-scatter.4
  197.8 83.2 all-gather.2
  290.3 50.2 reduce-scatter.2
  343.4 93.0 all-reduce.1
where the time goes:
time: 447 us
  waiting for transfers between devices  364 us (81%)
  matrix products  30.6 us (7%)
  other arithmetic  15 us (3%)
  starting transfers between devices  13.9 us (3%)
  between operations  13.8 us (3%)
  local copies, waits for them, and re-layouts  9.58 us (2%)
    ppermute x6, waiting for transfers between devices, partner_2(): lax.ppermute(shard, axis, [(i, i ^ 1 << distance) for i in range(lax.axis...  187 us
    all_gather x1, waiting for transfers between devices, body(): gathered = lax.all_gather(rotated, 'seq', axis=0, tiled=True)  79.5 us
    psum x1, waiting for transfers between devices, body(): lax.psum((grad_term * (1.0 / float(token_total) ** 0.5)).astype(jnp.bfloa...  39.6 us
    all_gather x1, waiting for transfers between devices, body(): grads_all = lax.all_gather(out_grad, 'tensor', axis=0, tiled=True)  36.3 us
    reduce_scatter x1, waiting for transfers between devices, body(): lax.psum_scatter(lax.dot_general(grads_all, weight, (((1,), (1,)), ((), (...  20.5 us
    ppermute x6, starting transfers between devices, partner_2(): lax.ppermute(shard, axis, [(i, i ^ 1 << distance) for i in range(lax.axis...  13.7 us
    dot_general x1, matrix products, body(): lax.dot_general(grads_all, weight, (((1,), (1,)), ((), ())), preferred_el...  9.3 us
    dot_general x1, matrix products, body(): partial_sums = jnp.dot(gathered, weight, preferred_element_type=jnp.float32)  9.08 us
  transfers between devices with their start and end apart: 11, of which 9 were waited for; matrix products, arithmetic and copies ran while one was open for 9% of the time, Pallas kernels for 0%

commit v1 on v0

--- a/solution.py
+++ b/solution.py
@@ -58,7 +58,8 @@
     output = lax.psum_scatter(
         partial_sums.astype(jnp.bfloat16), "tensor", scatter_dimension=0, tiled=True
     )
-    grads_all = lax.all_gather(out_grad, "tensor", axis=0, tiled=True)
+    sent = jnp.stack([out_grad] * lax.axis_size("tensor"))
+    grads_all = jnp.concatenate(lax.all_to_all(sent, "tensor", 0, 0), axis=0)
     token_total = hidden.shape[0] * lax.axis_size("seq") * lax.axis_size("dp")
     grad_term = lax.dot_general(
         gathered, grads_all, (((0,), (0,)), ((), ())), preferred_element_type=jnp.float32

time: 447 us -> 450 us (level)
  waiting for transfers between devices: 364 us -> 329 us
  blocking collectives: 0 us -> 34.7 us
    all_gather x1 -> x0, waiting for transfers between devices: 36.3 us -> none  [body(): grads_all = lax.all_gather(out_grad, 'tensor', axis=0, tiled=True)]
    all_to_all x0 -> x1, blocking collectives: none -> 34.7 us  [body(): grads_all = jnp.concatenate(lax.all_to_all(sent, 'tensor', 0, 0), axis=0)]
    unnamed x9 -> x11, local copies, waits for them, and re-layouts: 8.03 us -> 9 us
  transfers between devices with their start and end apart: 11 -> 10, of which waited for: 9 -> 8; matrix products, arithmetic and copies ran while one was open for 9% -> 9% of each run, Pallas kernels for 0% -> 0%
where the time goes in v1:
time: 450 us; the launch traced here: 449 us
  waiting for transfers between devices  329 us (73%)
  blocking collectives  34.7 us (8%)
  matrix products  29.7 us (7%)
  starting transfers between devices  15.7 us (3%)
  other arithmetic  15.1 us (3%)
  between operations  13.8 us (3%)
  local copies, waits for them, and re-layouts  11.5 us (3%)
    ppermute x6, waiting for transfers between devices, partner_2(): lax.ppermute(shard, axis, [(i, i ^ 1 << distance) for i in range(lax.axis...  189 us
    all_gather x1, waiting for transfers between devices, body(): gathered = lax.all_gather(rotated, 'seq', axis=0, tiled=True)  79.5 us
    psum x1, waiting for transfers between devices, body(): lax.psum((grad_term * (1.0 / float(token_total) ** 0.5)).astype(jnp.bfloa...  39.7 us
    all_to_all x1, blocking collectives, body(): grads_all = jnp.concatenate(lax.all_to_all(sent, 'tensor', 0, 0), axis=0)  34.7 us
    reduce_scatter x1, waiting for transfers between devices, body(): lax.psum_scatter(lax.dot_general(grads_all, weight, (((1,), (1,)), ((), (...  20.3 us
    ppermute x6, starting transfers between devices, partner_2(): lax.ppermute(shard, axis, [(i, i ^ 1 << distance) for i in range(lax.axis...  15.5 us
    dot_general x1, matrix products, body(): partial_sums = jnp.dot(gathered, weight, preferred_element_type=jnp.float32)  9.11 us
    unnamed x11, local copies, waits for them, and re-layouts  9 us
  transfers between devices with their start and end apart: 10, of which 8 were waited for; matrix products, arithmetic and copies ran while one was open for 9% of the time, Pallas kernels for 0%

profile of v1, /device:TPU:1, one launch (start us, length us, event | category | flops | bytes accessed | tf_op | source)
XLA Modules:
  0.0 449.2 jit_solution(4942421829117687060)
XLA Ops:
  7.2 0.0 reduce-scatter.5.cloned.1.call-start
  7.2 1.0 stack.2
  8.2 34.7 %all_to_all.5 = bf16[8,128,512]{2,1,0:T(8,128)(2,1)S(1)} all-to-all(bf16[8,128,512]{2,1,0:T(8,128)(2,1)S(1)} %stack.2), channel_id=1, replica_groups=mesh['dp'=4,'seq'=8,'tensor'=8] {'tensor'}, dimensions={0} | all-to-all | bytes 2097152 | tf_op jit(solution)/shard_map/all_to_all | solution.py:62
  42.9 1.0 copy-done
  43.9 8.3 %convolution_convert_fusion = bf16[1024,3584]{1,0:T(8,128)(2,1)} fusion(bf16[1024,512]{1,0:T(8,128)(2,1)S(1)} %bitcast.37, bf16[3584,512]{1,0:T(8,128)(2,1)} %param.4), kind=kOutput, calls=%fused_computation | convolution fusion | flops 3761766400 | bytes 12058624 | tf_op jit(solution)/shard_map/dot_general | solution.py:71
  52.2 0.0 reduce-scatter.5.cloned.1.call-update
  52.2 0.0 copy-start.3
  52.3 0.0 all-gather.2.cloned.1.call-start
  52.3 1.1 copy-done.2
  53.4 0.6 copy.11
  54.0 0.0 copy-done.3
  54.0 0.7 fusion.14
  54.7 1.0 bitcast_convert_fusion.1
  55.7 4.3 collective-permute-start
  60.0 2.3 collective-permute-done
  62.3 1.2 fusion.13
  63.6 0.6 collective-permute-start.1
  64.1 41.6 %collective-permute-done.1 = bf16[128,3584]{0,1:T(8,128)(2,1)} collective-permute-done((bf16[128,3584]{0,1:T(8,128)(2,1)}, bf16[128,3584]{0,1:T(8,128)(2,1)}, u32[]{:S(2)}, u32[]{:S(2)}) %collective-permute-start.1) | collective-permute-done | bytes 917536 | tf_op jit(solution)/shard_map/ppermute | solution.py:10
  105.7 2.6 fusion.11
  108.4 1.3 collective-permute-start.2
  109.6 63.9 %collective-permute-done.2 = bf16[128,3584]{0,1:T(8,128)(2,1)} collective-permute-done((bf16[128,3584]{0,1:T(8,128)(2,1)}, bf16[128,3584]{0,1:T(8,128)(2,1)}, u32[]{:S(2)}, u32[]{:S(2)}) %collective-permute-start.2) | collective-permute-done | bytes 917536 | tf_op jit(solution)/shard_map/ppermute | solution.py:10
  173.5 3.2 fusion.4
  176.7 0.0 all-gather.2.cloned.1.call-update
  176.7 0.0 reduce-scatter.3.cloned.1.call-start
  176.8 20.3 %reduce-scatter.5.cloned.1.call-done = bf16[128,3584]{1,0:T(8,128)(2,1)} async-done(((bf16[1024,3584]{1,0:T(8,128)(2,1)}), bf16[128,3584]{1,0:T(8,128)(2,1)}) %reduce-scatter.5.cloned.1.call-update) | async-done | bytes 917520 | tf_op jit(solution)/shard_map/reduce_scatter | solution.py:70
  197.1 1.5 copy.13
  198.7 3.1 fusion.15
  201.7 1.1 bitcast_convert_fusion
  202.8 0.7 collective-permute-start.3
  203.6 79.5 %all-gather.2.cloned.1.call-done = bf16[1024,3584]{0,1:T(8,128)(2,1)} async-done(((bf16[128,3584]{0,1:T(8,128)(2,1)}), bf16[1024,3584]{0,1:T(8,128)(2,1)}) %all-gather.2.cloned.1.call-update) | async-done | bytes 7340048 | tf_op jit(solution)/shard_map/all_gather | solution.py:56
  283.1 9.1 %convolution_convert_fusion.1 = bf16[1024,512]{1,0:T(8,128)(2,1)} fusion(bf16[1024,3584]{0,1:T(8,128)(2,1)} %all-gather.2.cloned.1.call-done, bf16[3584,512]{1,0:T(8,128)(2,1)} %param.4), kind=kOutput, calls=%fused_computation.26 | convolution fusion | flops 3758620672 | bytes 12058624 | tf_op jit(solution)/shard_map/dot_general | solution.py:57
  292.2 0.0 reduce-scatter.3.cloned.1.call-update
  292.2 0.0 all-reduce.2.cloned.1.call-start
  292.3 0.0 copy-start.1
  292.3 0.0 collective-permute-done.3
  292.3 1.2 fusion.12
  293.5 2.3 collective-permute-start.4
  295.8 0.0 copy-done.1
  295.8 8.5 %multiply_convert_fusion = bf16[3584,512]{1,0:T(8,128)(2,1)} fusion(bf16[1024,3584]{0,1:T(8,128)(2,1)} %all-gather.2.cloned.1.call-done, bf16[1024,512]{1,0:T(8,128)(2,1)S(1)} %bitcast.38), kind=kOutput, calls=%fused_computation.1 | convolution fusion | flops 3761766400 | bytes 12058624 | tf_op jit(solution)/shard_map/dot_general | solution.py:64
  304.2 0.0 all-reduce.2.cloned.1.call-update
  304.3 41.2 %collective-permute-done.4 = bf16[128,3584]{0,1:T(8,128)(2,1)} collective-permute-done((bf16[128,3584]{0,1:T(8,128)(2,1)}, bf16[128,3584]{0,1:T(8,128)(2,1)}, u32[]{:S(2)}, u32[]{:S(2)}) %collective-permute-start.4) | collective-permute-done | bytes 917536 | tf_op jit(solution)/shard_map/ppermute | solution.py:10
  345.5 1.7 fusion.10
  347.2 6.4 %collective-permute-start.5 = (bf16[128,3584]{0,1:T(8,128)(2,1)S(1)}, bf16[128,3584]{0,1:T(8,128)(2,1)S(1)}, u32[]{:S(2)}, u32[]{:S(2)}) collective-permute-start(bf16[128,3584]{0,1:T(8,128)(2,1)S(1)} %fusion.10), channel_id=1, source_target_pairs={{0,4},{1,5},{2,6},{3,7},{4,0},{5,1},{6,2},{7,3},{8,12},{9,13},{10,... | collective-permute-start | bytes 2752520 | tf_op jit(solution)/shard_map/ppermute | solution.py:10
  353.7 40.0 %collective-permute-done.5 = bf16[128,3584]{0,1:T(8,128)(2,1)S(1)} collective-permute-done((bf16[128,3584]{0,1:T(8,128)(2,1)S(1)}, bf16[128,3584]{0,1:T(8,128)(2,1)S(1)}, u32[]{:S(2)}, u32[]{:S(2)}) %collective-permute-start.5) | collective-permute-done | bytes 917536 | tf_op jit(solution)/shard_map/ppermute | solution.py:10
  393.6 3.0 fusion.9
  396.6 2.2 copy.16
  398.8 39.7 %all-reduce.2.cloned.1.call-done = bf16[3584,512]{1,0:T(8,128)(2,1)} async-done(((bf16[3584,512]{1,0:T(8,128)(2,1)}), bf16[3584,512]{1,0:T(8,128)(2,1)}) %all-reduce.2.cloned.1.call-update) | async-done | bytes 3670032 | tf_op jit(solution)/shard_map/psum | solution.py:67
  438.5 4.1 copy.21
  (3 shorter events, 0.0 us)
Async XLA Ops:
  7.2 190.0 %reduce-scatter.5.cloned.1.call-start = ((), (), s32[]{:S(2)}) async-start(), calls=%async_computation.5 | async-start | bytes 8257536 | tf_op jit(solution)/shard_map/reduce_scatter | solution.py:70
  42.9 1.0 copy-start
  52.2 1.2 copy-start.2
  52.2 1.8 copy-start.3
  52.3 230.8 %all-gather.2.cloned.1.call-start = ((), (), s32[]{:S(2)}) async-start(), calls=%async_computation.3 | async-start | bytes 8257536 | tf_op jit(solution)/shard_map/all_gather | solution.py:56
  55.7 6.6 %collective-permute-start = (bf16[128,3584]{0,1:T(8,128)(2,1)}, bf16[128,3584]{0,1:T(8,128)(2,1)S(1)}, u32[]{:S(2)}, u32[]{:S(2)}) collective-permute-start(bf16[128,3584]{0,1:T(8,128)(2,1)} %bitcast_convert_fusion.1), channel_id=1, source_target_pairs={{0,1},{1,0},{2,3},{3,2},{4,5},{5,4},{6,7},{7,6},{8,9},{9,8},{10,11... | collective-permute-start | bytes 2752520 | tf_op jit(solution)/shard_map/ppermute | solution.py:10
  63.6 42.1 %collective-permute-start.1 = (bf16[128,3584]{0,1:T(8,128)(2,1)}, bf16[128,3584]{0,1:T(8,128)(2,1)}, u32[]{:S(2)}, u32[]{:S(2)}) collective-permute-start(bf16[128,3584]{0,1:T(8,128)(2,1)} %fusion.13), channel_id=1, source_target_pairs={{0,2},{1,3},{2,0},{3,1},{4,6},{5,7},{6,4},{7,5},{8,10},{9,11},{10,... | collective-permute-start | bytes 2752520 | tf_op jit(solution)/shard_map/ppermute | solution.py:10
  108.4 65.1 %collective-permute-start.2 = (bf16[128,3584]{0,1:T(8,128)(2,1)}, bf16[128,3584]{0,1:T(8,128)(2,1)}, u32[]{:S(2)}, u32[]{:S(2)}) collective-permute-start(bf16[128,3584]{0,1:T(8,128)(2,1)} %fusion.11), channel_id=1, source_target_pairs={{0,4},{1,5},{2,6},{3,7},{4,0},{5,1},{6,2},{7,3},{8,12},{9,13},{10,... | collective-permute-start | bytes 2752520 | tf_op jit(solution)/shard_map/ppermute | solution.py:10
  176.7 222.1 %reduce-scatter.3.cloned.1.call-start = ((), (), s32[]{:S(2)}) async-start(), calls=%async_computation.4 | async-start | bytes 1179648 | tf_op jit(solution)/shard_map/reduce_scatter | solution.py:58
  202.8 89.4 %collective-permute-start.3 = (bf16[128,3584]{0,1:T(8,128)(2,1)}, bf16[128,3584]{0,1:T(8,128)(2,1)S(1)}, u32[]{:S(2)}, u32[]{:S(2)}) collective-permute-start(bf16[128,3584]{0,1:T(8,128)(2,1)} %bitcast_convert_fusion), channel_id=1, source_target_pairs={{0,1},{1,0},{2,3},{3,2},{4,5},{5,4},{6,7},{7,6},{8,9},{9,8},{10,11... | collective-permute-start | bytes 2752520 | tf_op jit(solution)/shard_map/ppermute | solution.py:10
  292.2 146.3 %all-reduce.2.cloned.1.call-start = ((), (), s32[]{:S(2)}) async-start(), calls=%async_computation.6 | async-start | bytes 7340032 | tf_op jit(solution)/shard_map/psum | solution.py:67
  292.3 3.5 copy-start.1
  293.5 52.0 %collective-permute-start.4 = (bf16[128,3584]{0,1:T(8,128)(2,1)}, bf16[128,3584]{0,1:T(8,128)(2,1)}, u32[]{:S(2)}, u32[]{:S(2)}) collective-permute-start(bf16[128,3584]{0,1:T(8,128)(2,1)} %fusion.12), channel_id=1, source_target_pairs={{0,2},{1,3},{2,0},{3,1},{4,6},{5,7},{6,4},{7,5},{8,10},{9,11},{10,... | collective-permute-start | bytes 2752520 | tf_op jit(solution)/shard_map/ppermute | solution.py:10
  347.2 46.4 %collective-permute-start.5 = (bf16[128,3584]{0,1:T(8,128)(2,1)S(1)}, bf16[128,3584]{0,1:T(8,128)(2,1)S(1)}, u32[]{:S(2)}, u32[]{:S(2)}) collective-permute-start(bf16[128,3584]{0,1:T(8,128)(2,1)S(1)} %fusion.10), channel_id=1, source_target_pairs={{0,4},{1,5},{2,6},{3,7},{4,0},{5,1},{6,2},{7,3},{8,12},{9,13},{10,... | collective-permute-start | bytes 2752520 | tf_op jit(solution)/shard_map/ppermute | solution.py:10
Sparse Core Ops, SparseCore 0:
  52.4 144.7 reduce-scatter.4
  199.4 83.6 all-gather.1
  292.3 50.2 reduce-scatter.2
  345.4 93.0 all-reduce.1
